TPU v7x, 512 devices: a whole 4x8x8 slice. The times are simulated.
512 devices in a mesh: rows: 128 (over z, y, core), cols: 4 (over x).
Axes of the slice: x: 4, y: 8, z: 8, core: 2. Of those that a mesh axis runs over, the one named last changes fastest.
Arguments:
- hidden_panel: float32 [8192, 16384], P('cols', 'rows'), may hold values from -6 to 6
- row_signs: float32 [16384], P('rows'), may hold values from -1 to 1, as said below
- sample_rows: int32 [128, 4], P('rows'), may hold values from 0 to 16383, as said below
- sample_counts: int32 [128], replicated, may hold values from 1 to 4, as said below
- ridge_weight: float32 [], replicated, may hold values from 0.5 to 2
Outputs:
- sketch_gram: float32 [8192, 8192], P('cols', 'rows')
Inputs may be any that keep to these rules, and one draw needn't show every extreme that they name: `sample_rows`: row p holds 4 distinct row numbers of p * 128 to (p + 1) * 128 - 1 in ascending order, so the whole array ascends; only the first sample_counts[p] of them are sampled, the rest are ignored. `sample_counts`: entry p counts the live slots of block p; some block has exactly 4. `row_signs`: every entry is +1 or -1.
All inputs are finite; a program needn't handle non-finite values.
Results may differ from a plain program's by a relative error of at most 0.00008.
Values sent between devices are 32-bit elements; how exact they have to be, the bound alone decides.
A program may use at most 64 MiB of HBM per device.

v0:
```python
import math
import jax
import jax.numpy as jnp
from jax import lax
from jax.sharding import PartitionSpec as P


def swapped(value, axis, bit):
    mask = 2**bit
    pairs = [(source, source ^ mask) for source in range(lax.axis_size(axis))]
    return lax.ppermute(value, axis, pairs)


def parity_signs(common, levels):
    parity = jnp.zeros_like(common)
    for bit_level in range(levels):
        parity = parity ^ common >> bit_level & 1
    return (1 - 2 * parity).astype(jnp.float32)


def sign_table(extent):
    positions = jnp.arange(extent, dtype=jnp.int32)
    return parity_signs(positions[:, None] & positions[None, :], extent.bit_length() - 1)


def local_transform(signed):
    width, length = signed.shape
    outer_size = min(128, length)
    inner_size = length // outer_size
    blocks = signed.reshape(width, outer_size, inner_size)
    blocks = jnp.einsum(
        "cab,ea->ceb", blocks, sign_table(outer_size), precision=lax.Precision.HIGHEST
    )
    blocks = jnp.einsum(
        "ceb,fb->cef", blocks, sign_table(inner_size), precision=lax.Precision.HIGHEST
    )
    return blocks.reshape(width, length)


def body(hidden_panel, row_signs, sample_rows, sample_counts, ridge_weight):
    width, length = hidden_panel.shape
    shards = lax.axis_size("rows")
    my_shard = lax.axis_index("rows")
    levels = shards.bit_length() - 1
    factor = 1.0 / math.sqrt(length * shards)
    slot_total = sample_rows.shape[1]
    spread = local_transform(hidden_panel * row_signs[None, :])
    for bit_level in range(levels):
        partner = swapped(spread, "rows", bit_level)
        upper_half = my_shard >> bit_level & 1 == 1
        spread = jnp.where(upper_half, partner - spread, spread + partner)
    picked = jnp.take(spread, sample_rows[0] - my_shard * length, axis=1) * factor
    live_slots = lax.dynamic_index_in_dim(sample_counts, my_shard, keepdims=False)
    slot_mask = (jnp.arange(slot_total) < live_slots).astype(jnp.float32)
    sketch = picked * slot_mask[None, :]
    all_slots = lax.all_gather(sketch, "rows", axis=1, tiled=True)
    all_units = lax.all_gather(sketch, "cols", axis=0, tiled=True)
    block_units = lax.all_to_all(all_units, "rows", split_axis=0, concat_axis=1, tiled=True)
    partial_value = jnp.dot(
        all_slots,
        block_units.T,
        precision=lax.Precision.HIGHEST,
        preferred_element_type=jnp.float32,
    )
    sample_total = jnp.sum(sample_counts).astype(jnp.float32)
    row_start = lax.axis_index("cols") * width
    block_width = block_units.shape[0]
    col_start = my_shard * block_width
    diagonal = (
        (row_start + jnp.arange(width))[:, None] == (col_start + jnp.arange(block_width))[None, :]
    ).astype(jnp.float32)
    return partial_value / sample_total + ridge_weight * diagonal


def solution(mesh):
    placed = (P("cols", "rows"), P("rows"), P("rows", None), P(), P())
    return jax.shard_map(
        body, mesh=mesh, in_specs=placed, out_specs=P("cols", "rows"), check_vma=False
    )
```

profile of v0, /device:TPU:1, one launch (start us, length us, event | category | flops | bytes accessed | tf_op | source)
XLA Modules:
  0.0 380.0 jit_solution(14253344918159398699)
XLA Ops:
  6.5 2.3 convolution_bitcast_fusion
  8.8 8.8 %collective-permute-start = (f32[2048,128]{0,1:T(8,128)S(1)}, f32[2048,128]{0,1:T(8,128)S(1)}, u32[]{:S(2)}, u32[]{:S(2)}) collective-permute-start(f32[2048,128]{0,1:T(8,128)S(1)} %convolution_bitcast_fusion), channel_id=1, source_target_pairs={{0,4},{4,0},{8,12},{12,8},{16,20},{20,16},{24,28},{28,24},{32,36},... | collective-permute-start | bytes 3145736 | tf_op jit(solution)/shard_map/ppermute | solution.py:11
  17.6 2.3 collective-permute-done
  20.0 1.9 collective-permute-start.1
  22.0 24.3 %collective-permute-done.1 = f32[2048,128]{0,1:T(8,128)S(1)} collective-permute-done((f32[2048,128]{0,1:T(8,128)S(1)}, f32[2048,128]{0,1:T(8,128)S(1)}, u32[]{:S(2)}, u32[]{:S(2)}) %collective-permute-start.1) | collective-permute-done | bytes 1048608 | tf_op jit(solution)/shard_map/ppermute | solution.py:11
  46.5 1.9 collective-permute-start.2
  48.4 48.4 %collective-permute-done.2 = f32[2048,128]{0,1:T(8,128)S(1)} collective-permute-done((f32[2048,128]{0,1:T(8,128)S(1)}, f32[2048,128]{0,1:T(8,128)S(1)}, u32[]{:S(2)}, u32[]{:S(2)}) %collective-permute-start.2) | collective-permute-done | bytes 1048608 | tf_op jit(solution)/shard_map/ppermute | solution.py:11
  96.9 2.0 collective-permute-start.3
  99.0 47.9 %collective-permute-done.3 = f32[2048,128]{0,1:T(8,128)S(1)} collective-permute-done((f32[2048,128]{0,1:T(8,128)S(1)}, f32[2048,128]{0,1:T(8,128)S(1)}, u32[]{:S(2)}, u32[]{:S(2)}) %collective-permute-start.3) | collective-permute-done | bytes 1048608 | tf_op jit(solution)/shard_map/ppermute | solution.py:11
  147.0 1.9 collective-permute-start.4
  148.9 23.2 %collective-permute-done.4 = f32[2048,128]{0,1:T(8,128)S(1)} collective-permute-done((f32[2048,128]{0,1:T(8,128)S(1)}, f32[2048,128]{0,1:T(8,128)S(1)}, u32[]{:S(2)}, u32[]{:S(2)}) %collective-permute-start.4) | collective-permute-done | bytes 1048608 | tf_op jit(solution)/shard_map/ppermute | solution.py:11
  172.2 4.7 %collective-permute-start.5 = (f32[2048,128]{0,1:T(8,128)S(1)}, f32[2048,128]{0,1:T(8,128)S(1)}, u32[]{:S(2)}, u32[]{:S(2)}) collective-permute-start(f32[2048,128]{0,1:T(8,128)S(1)} %add_select_fusion.2), channel_id=1, source_target_pairs={{0,128},{4,132},{8,136},{12,140},{16,144},{20,148},{24,152},{28,15... | collective-permute-start | bytes 3145736 | tf_op jit(solution)/shard_map/ppermute | solution.py:11
  176.9 45.1 %collective-permute-done.5 = f32[2048,128]{0,1:T(8,128)S(1)} collective-permute-done((f32[2048,128]{0,1:T(8,128)S(1)}, f32[2048,128]{0,1:T(8,128)S(1)}, u32[]{:S(2)}, u32[]{:S(2)}) %collective-permute-start.5) | collective-permute-done | bytes 1048608 | tf_op jit(solution)/shard_map/ppermute | solution.py:11
  222.2 8.2 %collective-permute-start.6 = (f32[2048,128]{0,1:T(8,128)S(1)}, f32[2048,128]{0,1:T(8,128)S(1)}, u32[]{:S(2)}, u32[]{:S(2)}) collective-permute-start(f32[2048,128]{0,1:T(8,128)S(1)} %add_select_fusion.1), channel_id=1, source_target_pairs={{0,256},{4,260},{8,264},{12,268},{16,272},{20,276},{24,280},{28,28... | collective-permute-start | bytes 3145736 | tf_op jit(solution)/shard_map/ppermute | solution.py:11
  231.6 43.6 %collective-permute-done.6 = f32[2048,128]{0,1:T(8,128)S(1)} collective-permute-done((f32[2048,128]{0,1:T(8,128)S(1)}, f32[2048,128]{0,1:T(8,128)S(1)}, u32[]{:S(2)}, u32[]{:S(2)}) %collective-permute-start.6) | collective-permute-done | bytes 1048608 | tf_op jit(solution)/shard_map/ppermute | solution.py:11
  275.9 0.7 fusion.37
  276.6 9.5 %all_gather.7 = f32[8192,4]{0,1:T(4,128)S(1)} all-gather(f32[2048,4]{0,1:T(4,128)S(1)} %get-tuple-element.5), channel_id=1, replica_groups=mesh['rows'=128,'cols'=4] {'cols'}, dimensions={0}, use_global_device_ids=true | all-gather | bytes 163840 | tf_op jit(solution)/shard_map/all_gather | solution.py:57
  286.5 0.9 reshape.65
  287.4 15.0 %all-to-all-start = ((f32[128,1,256]{2,1,0:T(1,128)}), f32[128,1,256]{2,1,0:T(1,128)S(1)}, u32[]{:S(2)}, u32[]{:S(2)}) async-start(f32[128,1,256]{2,1,0:T(1,128)} %reshape.65), calls=%async_computation | async-start | bytes 262144 | tf_op jit(solution)/shard_map/all_to_all | solution.py:58
  304.3 11.1 %all-to-all-done = f32[128,1,256]{2,1,0:T(1,128)S(1)} async-done(((f32[128,1,256]{2,1,0:T(1,128)}), f32[128,1,256]{2,1,0:T(1,128)S(1)}, u32[]{:S(2)}, u32[]{:S(2)}) %all-to-all-start) | async-done | bytes 131104 | tf_op jit(solution)/shard_map/all_to_all | solution.py:58
  315.9 1.0 reduce
  317.0 45.1 %all-gather.3.cloned.1.call-done = f32[128,4,2048]{2,1,0:T(4,128)} async-done(((f32[1,4,2048]{2,1,0:T(4,128)}), f32[128,4,2048]{2,1,0:T(4,128)}) %all-gather.3.cloned.1.call-update) | async-done | bytes 4194320 | tf_op jit(solution)/shard_map/all_gather | solution.py:56
  362.1 5.3 %reshape.64 = f32[512,2048]{1,0:T(8,128)} reshape(f32[128,4,2048]{2,1,0:T(4,128)} %all-gather.3.cloned.1.call-done) | data formatting | bytes 8388608
  367.4 5.8 %fusion = f32[2048,64]{0,1:T(8,128)} fusion(f32[512,2048]{1,0:T(8,128)} %reshape.64, f32[64,512]{0,1:T(8,128)S(1)} %bitcast.28, f32[]{:T(128)S(6)} %copy.10, s32[2048]{0:T(1024)S(1)} %iota_add_fusion, f32[]{:T(128)S(6)} %convert_element_type.13, s32[64]{0:T(128)S(1)} %iota_add_fusion.1), kind=kOutput, calls=%fused_computation.3 | convolution fusion | flops 805830656 | bytes 4858120 | tf_op jit(solution)/shard_map/dot_general | solution.py:59
  (26 shorter events, 4.6 us)
Async XLA Ops:
  6.5 355.6 %all-gather.3.cloned.1.call-start = ((), (), s32[]{:S(2)}) async-start(), calls=%async_computation.1 | async-start | bytes 4227072 | tf_op jit(solution)/shard_map/all_gather | solution.py:56
  8.8 11.1 %collective-permute-start = (f32[2048,128]{0,1:T(8,128)S(1)}, f32[2048,128]{0,1:T(8,128)S(1)}, u32[]{:S(2)}, u32[]{:S(2)}) collective-permute-start(f32[2048,128]{0,1:T(8,128)S(1)} %convolution_bitcast_fusion), channel_id=1, source_target_pairs={{0,4},{4,0},{8,12},{12,8},{16,20},{20,16},{24,28},{28,24},{32,36},... | collective-permute-start | bytes 3145736 | tf_op jit(solution)/shard_map/ppermute | solution.py:11
  20.0 26.3 %collective-permute-start.1 = (f32[2048,128]{0,1:T(8,128)S(1)}, f32[2048,128]{0,1:T(8,128)S(1)}, u32[]{:S(2)}, u32[]{:S(2)}) collective-permute-start(f32[2048,128]{0,1:T(8,128)S(1)} %add_select_fusion.6), channel_id=1, source_target_pairs={{0,8},{4,12},{8,0},{12,4},{16,24},{20,28},{24,16},{28,20},{32,40},... | collective-permute-start | bytes 3145736 | tf_op jit(solution)/shard_map/ppermute | solution.py:11
  46.5 50.3 %collective-permute-start.2 = (f32[2048,128]{0,1:T(8,128)S(1)}, f32[2048,128]{0,1:T(8,128)S(1)}, u32[]{:S(2)}, u32[]{:S(2)}) collective-permute-start(f32[2048,128]{0,1:T(8,128)S(1)} %add_select_fusion.5), channel_id=1, source_target_pairs={{0,16},{4,20},{8,24},{12,28},{16,0},{20,4},{24,8},{28,12},{32,48},... | collective-permute-start | bytes 3145736 | tf_op jit(solution)/shard_map/ppermute | solution.py:11
  96.9 49.9 %collective-permute-start.3 = (f32[2048,128]{0,1:T(8,128)S(1)}, f32[2048,128]{0,1:T(8,128)S(1)}, u32[]{:S(2)}, u32[]{:S(2)}) collective-permute-start(f32[2048,128]{0,1:T(8,128)S(1)} %add_select_fusion.4), channel_id=1, source_target_pairs={{0,32},{4,36},{8,40},{12,44},{16,48},{20,52},{24,56},{28,60},{32,0... | collective-permute-start | bytes 3145736 | tf_op jit(solution)/shard_map/ppermute | solution.py:11
  98.9 131.4 %copy-start.1 = (s32[128]{0:T(128)S(1)}, s32[128]{0:T(128)}, u32[]{:S(2)}) copy-start(s32[128]{0:T(128)} %param.8) | copy-start | bytes 1540
  98.9 132.7 %copy-start = (s32[1,4]{1,0:T(1,128)S(1)}, s32[1,4]{1,0:T(1,128)}, u32[]{:S(2)}) copy-start(s32[1,4]{1,0:T(1,128)} %param.7) | copy-start | bytes 52
  147.0 25.1 %collective-permute-start.4 = (f32[2048,128]{0,1:T(8,128)S(1)}, f32[2048,128]{0,1:T(8,128)S(1)}, u32[]{:S(2)}, u32[]{:S(2)}) collective-permute-start(f32[2048,128]{0,1:T(8,128)S(1)} %add_select_fusion.3), channel_id=1, source_target_pairs={{0,64},{4,68},{8,72},{12,76},{16,80},{20,84},{24,88},{28,92},{32,9... | collective-permute-start | bytes 3145736 | tf_op jit(solution)/shard_map/ppermute | solution.py:11
  172.2 49.8 %collective-permute-start.5 = (f32[2048,128]{0,1:T(8,128)S(1)}, f32[2048,128]{0,1:T(8,128)S(1)}, u32[]{:S(2)}, u32[]{:S(2)}) collective-permute-start(f32[2048,128]{0,1:T(8,128)S(1)} %add_select_fusion.2), channel_id=1, source_target_pairs={{0,128},{4,132},{8,136},{12,140},{16,144},{20,148},{24,152},{28,15... | collective-permute-start | bytes 3145736 | tf_op jit(solution)/shard_map/ppermute | solution.py:11
  222.2 53.0 %collective-permute-start.6 = (f32[2048,128]{0,1:T(8,128)S(1)}, f32[2048,128]{0,1:T(8,128)S(1)}, u32[]{:S(2)}, u32[]{:S(2)}) collective-permute-start(f32[2048,128]{0,1:T(8,128)S(1)} %add_select_fusion.1), channel_id=1, source_target_pairs={{0,256},{4,260},{8,264},{12,268},{16,272},{20,276},{24,280},{28,28... | collective-permute-start | bytes 3145736 | tf_op jit(solution)/shard_map/ppermute | solution.py:11
  287.4 28.0 %all-to-all-start = ((f32[128,1,256]{2,1,0:T(1,128)}), f32[128,1,256]{2,1,0:T(1,128)S(1)}, u32[]{:S(2)}, u32[]{:S(2)}) async-start(f32[128,1,256]{2,1,0:T(1,128)} %reshape.65), calls=%async_computation | async-start | bytes 262144 | tf_op jit(solution)/shard_map/all_to_all | solution.py:58
Sparse Core Ops, SparseCore 0:
  276.8 85.2 all-gather.2
where the time goes:
time: 381 us; the launch traced here: 380 us
  waiting for transfers between devices  291 us (76%)
  starting transfers between devices  44.5 us (12%)
  between operations  14.9 us (4%)
  blocking collectives  9.46 us (2%)
  local copies, waits for them, and re-layouts  8.41 us (2%)
  matrix products  8.04 us (2%)
  other arithmetic  3.98 us (1%)
    ppermute x7, waiting for transfers between devices, swapped(): return lax.ppermute(value, axis, pairs)  235 us
    all_gather x1, waiting for transfers between devices, body(): all_slots = lax.all_gather(sketch, 'rows', axis=1, tiled=True)  45.1 us
    ppermute x7, starting transfers between devices, swapped(): return lax.ppermute(value, axis, pairs)  29.4 us
    all_to_all x1, starting transfers between devices, body(): lax.all_to_all(all_units, 'rows', split_axis=0, concat_axis=1, tiled=True)  15 us
    all_to_all x1, waiting for transfers between devices, body(): lax.all_to_all(all_units, 'rows', split_axis=0, concat_axis=1, tiled=True)  11.1 us
    all_gather x1, blocking collectives, body(): all_units = lax.all_gather(sketch, 'cols', axis=0, tiled=True)  9.46 us
  transfers between devices with their start and end apart: 9, of which 9 were waited for; matrix products, arithmetic and copies ran while one was open for 1% of the time, Pallas kernels for 0%

commit v1 on v0

--- a/solution.py
+++ b/solution.py
@@ -55,7 +55,12 @@
     sketch = picked * slot_mask[None, :]
     all_slots = lax.all_gather(sketch, "rows", axis=1, tiled=True)
     all_units = lax.all_gather(sketch, "cols", axis=0, tiled=True)
-    block_units = lax.all_to_all(all_units, "rows", split_axis=0, concat_axis=1, tiled=True)
+    block_units = jnp.concatenate(
+        lax.all_to_all(
+            jnp.stack(jnp.split(all_units, lax.axis_size("rows"), axis=0)), "rows", 0, 0
+        ),
+        axis=1,
+    )
     partial_value = jnp.dot(
         all_slots,
         block_units.T,

time: 381 us -> 381 us (level)
  local copies, waits for them, and re-layouts: 8.41 us -> 13.5 us
  waiting for transfers between devices: 291 us -> 286 us
    unnamed x7 -> x134, local copies, waits for them, and re-layouts: 6.38 us -> 11.7 us
    all_gather x1, waiting for transfers between devices: 45.1 us -> 40.7 us  [body(): all_slots = lax.all_gather(sketch, 'rows', axis=1, tiled=True)]
  transfers between devices with their start and end apart: 9 -> 9, of which waited for: 9 -> 9; matrix products, arithmetic and copies ran while one was open for 1% -> 3% of each run, Pallas kernels for 0% -> 0%
where the time goes in v1:
time: 381 us; the launch traced here: 380 us
  waiting for transfers between devices  286 us (75%)
  starting transfers between devices  44.5 us (12%)
  between operations  14.9 us (4%)
  local copies, waits for them, and re-layouts  13.5 us (4%)
  blocking collectives  9.46 us (2%)
  matrix products  8.04 us (2%)
  other arithmetic  3.98 us (1%)
    ppermute x7, waiting for transfers between devices, swapped(): return lax.ppermute(value, axis, pairs)  235 us
    all_gather x1, waiting for transfers between devices, body(): all_slots = lax.all_gather(sketch, 'rows', axis=1, tiled=True)  40.7 us
    ppermute x7, starting transfers between devices, swapped(): return lax.ppermute(value, axis, pairs)  29.4 us
    all_to_all x1, starting transfers between devices, body(): lax.all_to_all(jnp.stack(jnp.split(all_units, lax.axis_size('rows'), axis...  15 us
    unnamed x134, local copies, waits for them, and re-layouts  11.7 us
    all_to_all x1, waiting for transfers between devices, body(): lax.all_to_all(jnp.stack(jnp.split(all_units, lax.axis_size('rows'), axis...  10.8 us
    all_gather x1, blocking collectives, body(): all_units = lax.all_gather(sketch, 'cols', axis=0, tiled=True)  9.46 us
  transfers between devices with their start and end apart: 9, of which 9 were waited for; matrix products, arithmetic and copies ran while one was open for 3% of the time, Pallas kernels for 0%

profile of v1, /device:TPU:1, one launch (start us, length us, event | category | flops | bytes accessed | tf_op | source)
XLA Modules:
  0.0 380.5 jit_solution(3538021883850363221)
XLA Ops:
  6.5 2.3 convolution_bitcast_fusion
  8.8 8.8 %collective-permute-start = (f32[2048,128]{0,1:T(8,128)S(1)}, f32[2048,128]{0,1:T(8,128)S(1)}, u32[]{:S(2)}, u32[]{:S(2)}) collective-permute-start(f32[2048,128]{0,1:T(8,128)S(1)} %convolution_bitcast_fusion), channel_id=1, source_target_pairs={{0,4},{4,0},{8,12},{12,8},{16,20},{20,16},{24,28},{28,24},{32,36},... | collective-permute-start | bytes 3145736 | tf_op jit(solution)/shard_map/ppermute | solution.py:11
  17.6 2.3 collective-permute-done
  20.0 1.9 collective-permute-start.1
  22.0 24.3 %collective-permute-done.1 = f32[2048,128]{0,1:T(8,128)S(1)} collective-permute-done((f32[2048,128]{0,1:T(8,128)S(1)}, f32[2048,128]{0,1:T(8,128)S(1)}, u32[]{:S(2)}, u32[]{:S(2)}) %collective-permute-start.1) | collective-permute-done | bytes 1048608 | tf_op jit(solution)/shard_map/ppermute | solution.py:11
  46.5 1.9 collective-permute-start.2
  48.4 48.4 %collective-permute-done.2 = f32[2048,128]{0,1:T(8,128)S(1)} collective-permute-done((f32[2048,128]{0,1:T(8,128)S(1)}, f32[2048,128]{0,1:T(8,128)S(1)}, u32[]{:S(2)}, u32[]{:S(2)}) %collective-permute-start.2) | collective-permute-done | bytes 1048608 | tf_op jit(solution)/shard_map/ppermute | solution.py:11
  96.9 2.0 collective-permute-start.3
  99.0 47.9 %collective-permute-done.3 = f32[2048,128]{0,1:T(8,128)S(1)} collective-permute-done((f32[2048,128]{0,1:T(8,128)S(1)}, f32[2048,128]{0,1:T(8,128)S(1)}, u32[]{:S(2)}, u32[]{:S(2)}) %collective-permute-start.3) | collective-permute-done | bytes 1048608 | tf_op jit(solution)/shard_map/ppermute | solution.py:11
  147.0 1.9 collective-permute-start.4
  148.9 23.2 %collective-permute-done.4 = f32[2048,128]{0,1:T(8,128)S(1)} collective-permute-done((f32[2048,128]{0,1:T(8,128)S(1)}, f32[2048,128]{0,1:T(8,128)S(1)}, u32[]{:S(2)}, u32[]{:S(2)}) %collective-permute-start.4) | collective-permute-done | bytes 1048608 | tf_op jit(solution)/shard_map/ppermute | solution.py:11
  172.2 4.7 %collective-permute-start.5 = (f32[2048,128]{0,1:T(8,128)S(1)}, f32[2048,128]{0,1:T(8,128)S(1)}, u32[]{:S(2)}, u32[]{:S(2)}) collective-permute-start(f32[2048,128]{0,1:T(8,128)S(1)} %add_select_fusion.2), channel_id=1, source_target_pairs={{0,128},{4,132},{8,136},{12,140},{16,144},{20,148},{24,152},{28,15... | collective-permute-start | bytes 3145736 | tf_op jit(solution)/shard_map/ppermute | solution.py:11
  176.9 45.1 %collective-permute-done.5 = f32[2048,128]{0,1:T(8,128)S(1)} collective-permute-done((f32[2048,128]{0,1:T(8,128)S(1)}, f32[2048,128]{0,1:T(8,128)S(1)}, u32[]{:S(2)}, u32[]{:S(2)}) %collective-permute-start.5) | collective-permute-done | bytes 1048608 | tf_op jit(solution)/shard_map/ppermute | solution.py:11
  222.2 8.2 %collective-permute-start.6 = (f32[2048,128]{0,1:T(8,128)S(1)}, f32[2048,128]{0,1:T(8,128)S(1)}, u32[]{:S(2)}, u32[]{:S(2)}) collective-permute-start(f32[2048,128]{0,1:T(8,128)S(1)} %add_select_fusion.1), channel_id=1, source_target_pairs={{0,256},{4,260},{8,264},{12,268},{16,272},{20,276},{24,280},{28,28... | collective-permute-start | bytes 3145736 | tf_op jit(solution)/shard_map/ppermute | solution.py:11
  231.6 43.6 %collective-permute-done.6 = f32[2048,128]{0,1:T(8,128)S(1)} collective-permute-done((f32[2048,128]{0,1:T(8,128)S(1)}, f32[2048,128]{0,1:T(8,128)S(1)}, u32[]{:S(2)}, u32[]{:S(2)}) %collective-permute-start.6) | collective-permute-done | bytes 1048608 | tf_op jit(solution)/shard_map/ppermute | solution.py:11
  275.9 0.7 fusion.37
  276.6 9.5 %all_gather.7 = f32[8192,4]{0,1:T(4,128)S(1)} all-gather(f32[2048,4]{0,1:T(4,128)S(1)} %get-tuple-element.5), channel_id=1, replica_groups=mesh['rows'=128,'cols'=4] {'cols'}, dimensions={0}, use_global_device_ids=true | all-gather | bytes 163840 | tf_op jit(solution)/shard_map/all_gather | solution.py:57
  291.6 0.9 reshape.70
  292.5 15.0 %all-to-all-start = ((f32[128,1,256]{2,1,0:T(1,128)}), f32[128,1,256]{2,1,0:T(1,128)S(1)}, u32[]{:S(2)}, u32[]{:S(2)}) async-start(f32[128,1,256]{2,1,0:T(1,128)} %reshape.70), calls=%async_computation | async-start | bytes 262144 | tf_op jit(solution)/shard_map/all_to_all | solution.py:59
  309.4 10.8 %all-to-all-done = f32[128,1,256]{2,1,0:T(1,128)S(1)} async-done(((f32[128,1,256]{2,1,0:T(1,128)}), f32[128,1,256]{2,1,0:T(1,128)S(1)}, u32[]{:S(2)}, u32[]{:S(2)}) %all-to-all-start) | async-done | bytes 131104 | tf_op jit(solution)/shard_map/all_to_all | solution.py:59
  320.7 1.0 reduce
  321.8 40.7 %all-gather.3.cloned.1.call-done = f32[128,4,2048]{2,1,0:T(4,128)} async-done(((f32[1,4,2048]{2,1,0:T(4,128)}), f32[128,4,2048]{2,1,0:T(4,128)}) %all-gather.3.cloned.1.call-update) | async-done | bytes 4194320 | tf_op jit(solution)/shard_map/all_gather | solution.py:56
  362.6 5.3 %reshape.69 = f32[512,2048]{1,0:T(8,128)} reshape(f32[128,4,2048]{2,1,0:T(4,128)} %all-gather.3.cloned.1.call-done) | data formatting | bytes 8388608
  367.9 5.8 %fusion = f32[2048,64]{0,1:T(8,128)} fusion(f32[512,2048]{1,0:T(8,128)} %reshape.69, f32[64,512]{0,1:T(8,128)S(1)} %bitcast.536, f32[]{:T(128)S(6)} %copy.133, s32[2048]{0:T(1024)S(1)} %iota_add_fusion, f32[]{:T(128)S(6)} %convert_element_type.13, s32[64]{0:T(128)S(1)} %iota_add_fusion.1), kind=kOutput, calls=%fused_computation.3 | convolution fusion | flops 805830656 | bytes 4858120 | tf_op jit(solution)/shard_map/dot_general | solution.py:64
  (152 shorter events, 9.6 us)
Async XLA Ops:
  6.5 356.0 %all-gather.3.cloned.1.call-start = ((), (), s32[]{:S(2)}) async-start(), calls=%async_computation.1 | async-start | bytes 4227072 | tf_op jit(solution)/shard_map/all_gather | solution.py:56
  8.8 11.1 %collective-permute-start = (f32[2048,128]{0,1:T(8,128)S(1)}, f32[2048,128]{0,1:T(8,128)S(1)}, u32[]{:S(2)}, u32[]{:S(2)}) collective-permute-start(f32[2048,128]{0,1:T(8,128)S(1)} %convolution_bitcast_fusion), channel_id=1, source_target_pairs={{0,4},{4,0},{8,12},{12,8},{16,20},{20,16},{24,28},{28,24},{32,36},... | collective-permute-start | bytes 3145736 | tf_op jit(solution)/shard_map/ppermute | solution.py:11
  20.0 26.3 %collective-permute-start.1 = (f32[2048,128]{0,1:T(8,128)S(1)}, f32[2048,128]{0,1:T(8,128)S(1)}, u32[]{:S(2)}, u32[]{:S(2)}) collective-permute-start(f32[2048,128]{0,1:T(8,128)S(1)} %add_select_fusion.6), channel_id=1, source_target_pairs={{0,8},{4,12},{8,0},{12,4},{16,24},{20,28},{24,16},{28,20},{32,40},... | collective-permute-start | bytes 3145736 | tf_op jit(solution)/shard_map/ppermute | solution.py:11
  46.5 50.3 %collective-permute-start.2 = (f32[2048,128]{0,1:T(8,128)S(1)}, f32[2048,128]{0,1:T(8,128)S(1)}, u32[]{:S(2)}, u32[]{:S(2)}) collective-permute-start(f32[2048,128]{0,1:T(8,128)S(1)} %add_select_fusion.5), channel_id=1, source_target_pairs={{0,16},{4,20},{8,24},{12,28},{16,0},{20,4},{24,8},{28,12},{32,48},... | collective-permute-start | bytes 3145736 | tf_op jit(solution)/shard_map/ppermute | solution.py:11
  96.9 49.9 %collective-permute-start.3 = (f32[2048,128]{0,1:T(8,128)S(1)}, f32[2048,128]{0,1:T(8,128)S(1)}, u32[]{:S(2)}, u32[]{:S(2)}) collective-permute-start(f32[2048,128]{0,1:T(8,128)S(1)} %add_select_fusion.4), channel_id=1, source_target_pairs={{0,32},{4,36},{8,40},{12,44},{16,48},{20,52},{24,56},{28,60},{32,0... | collective-permute-start | bytes 3145736 | tf_op jit(solution)/shard_map/ppermute | solution.py:11
  98.9 131.4 %copy-start.1 = (s32[128]{0:T(128)S(1)}, s32[128]{0:T(128)}, u32[]{:S(2)}) copy-start(s32[128]{0:T(128)} %param.8) | copy-start | bytes 1540
  98.9 132.7 %copy-start = (s32[1,4]{1,0:T(1,128)S(1)}, s32[1,4]{1,0:T(1,128)}, u32[]{:S(2)}) copy-start(s32[1,4]{1,0:T(1,128)} %param.7) | copy-start | bytes 52
  147.0 25.1 %collective-permute-start.4 = (f32[2048,128]{0,1:T(8,128)S(1)}, f32[2048,128]{0,1:T(8,128)S(1)}, u32[]{:S(2)}, u32[]{:S(2)}) collective-permute-start(f32[2048,128]{0,1:T(8,128)S(1)} %add_select_fusion.3), channel_id=1, source_target_pairs={{0,64},{4,68},{8,72},{12,76},{16,80},{20,84},{24,88},{28,92},{32,9... | collective-permute-start | bytes 3145736 | tf_op jit(solution)/shard_map/ppermute | solution.py:11
  172.2 49.8 %collective-permute-start.5 = (f32[2048,128]{0,1:T(8,128)S(1)}, f32[2048,128]{0,1:T(8,128)S(1)}, u32[]{:S(2)}, u32[]{:S(2)}) collective-permute-start(f32[2048,128]{0,1:T(8,128)S(1)} %add_select_fusion.2), channel_id=1, source_target_pairs={{0,128},{4,132},{8,136},{12,140},{16,144},{20,148},{24,152},{28,15... | collective-permute-start | bytes 3145736 | tf_op jit(solution)/shard_map/ppermute | solution.py:11
  222.2 53.0 %collective-permute-start.6 = (f32[2048,128]{0,1:T(8,128)S(1)}, f32[2048,128]{0,1:T(8,128)S(1)}, u32[]{:S(2)}, u32[]{:S(2)}) collective-permute-start(f32[2048,128]{0,1:T(8,128)S(1)} %add_select_fusion.1), channel_id=1, source_target_pairs={{0,256},{4,260},{8,264},{12,268},{16,272},{20,276},{24,280},{28,28... | collective-permute-start | bytes 3145736 | tf_op jit(solution)/shard_map/ppermute | solution.py:11
  292.5 27.7 %all-to-all-start = ((f32[128,1,256]{2,1,0:T(1,128)}), f32[128,1,256]{2,1,0:T(1,128)S(1)}, u32[]{:S(2)}, u32[]{:S(2)}) async-start(f32[128,1,256]{2,1,0:T(1,128)} %reshape.70), calls=%async_computation | async-start | bytes 262144 | tf_op jit(solution)/shard_map/all_to_all | solution.py:59
Sparse Core Ops, SparseCore 0:
  276.8 85.7 all-gather.2
